TPU v7x, 128 devices: a whole 4x4x4 slice. The times are simulated.
128 devices in a mesh: sx: 8 (over y, core), sy: 16 (over x, z).
Axes of the slice: x: 4, y: 4, z: 4, core: 2. Of those that a mesh axis runs over, the one named last changes fastest.
Arguments:
- loads: float32 [8, 16, 1536, 256], P('sx', 'sy')
- schur_flex: float32 [8, 16, 1536, 1536], P('sx', 'sy'), as said below
- dirichlet: float32 [8, 16, 1536, 1536], P('sx', 'sy'), as said below
- coupling: float32 [8, 16, 16, 1536], P('sx', 'sy'), may hold values from -0.3125 to 0.3125
- corner_index: int32 [8, 16, 16], P('sx', 'sy'), may hold values from 0 to 512, as said below
- face_lists: int32 [8, 16, 4, 384], P('sx', 'sy'), may hold values from 0 to 383, as said below
- coarse_inverse: float32 [512, 512], P(('sx', 'sy')), as said below
Outputs:
- multipliers: float32 [8, 16, 1536, 256], P('sx', 'sy')
- residual: float32 [8, 16, 1536, 256], P('sx', 'sy')
Inputs may be any that keep to these rules, and one draw needn't show every extreme that they name: `corner_index`: each subdomain lists 4 coarse dofs for each of its four corners; 512 marks a corner on the clamped edges of the panel, which has no coarse dof; every coarse dof below 512 is named by some subdomain. `face_lists`: each face's list is a permutation of the 384 dofs of the facing face; the facing lists of two neighbouring subdomains are inverse permutations. `schur_flex`: symmetric positive definite for every subdomain. `dirichlet`: symmetric positive definite for every subdomain. `coarse_inverse`: symmetric positive definite.
All inputs are finite; a program needn't handle non-finite values.
Results may differ from a plain program's by a relative error of at most 0.00017.
Values sent between devices are 32-bit elements; how exact they have to be, the bound alone decides.
A program may use at most 128 MiB of HBM per device.

v0:
```python
import jax
import jax.numpy as jnp
from jax import lax
from jax.sharding import PartitionSpec as P

HIGH = lax.Precision.HIGH
HIGHEST = lax.Precision.HIGHEST


def shifted(block, axis, distance):
    devices = range(lax.axis_size(axis))
    route = [(i - distance, i) for i in devices if i - distance in devices]
    return lax.ppermute(block, axis, route)


def facing(faces):
    return (
        shifted(faces[1], "sx", 1),
        shifted(faces[0], "sx", -1),
        shifted(faces[3], "sy", 1),
        shifted(faces[2], "sy", -1),
    )


def jump(field, match):
    size = field.shape[0] // 4
    faces = [field[f * size : (f + 1) * size] for f in range(4)]
    received = facing(faces)
    return jnp.concatenate(
        [faces[f] - jnp.dot(match[f], received[f], precision=HIGHEST) for f in range(4)], axis=0
    )


def inner(first, second):
    return jnp.sum(first * second, axis=0)


def shards(loads, schur_flex, dirichlet, coupling, corner_index, face_lists, coarse_inverse):
    flex_mat = schur_flex[0, 0]
    prec_mat = dirichlet[0, 0]
    coupling_mat = coupling[0, 0]
    corners = corner_index[0, 0]
    face_index = face_lists[0, 0]
    ncoarse = coarse_inverse.shape[1]
    ncl = corners.shape[0]
    size = face_index.shape[1]
    sx = lax.axis_index("sx")
    sy = lax.axis_index("sy")
    inside = jnp.stack([sx > 0, sx < lax.axis_size("sx") - 1, sy > 0, sy < lax.axis_size("sy") - 1])
    scale = jnp.repeat(1.0 + inside.astype(jnp.float32), size)[:, None]
    match = (face_index[:, :, None] == jnp.arange(size, dtype=jnp.int32)[None, None, :]).astype(
        jnp.float32
    )
    inverse = lax.all_gather(coarse_inverse, ("sx", "sy"), axis=0, tiled=True)
    slots = jnp.concatenate([corners, jnp.arange(ncoarse + 1, ncoarse + 4, dtype=jnp.int32)])
    place = (slots[None, :] == jnp.arange(ncoarse + 8, dtype=jnp.int32)[:, None]).astype(
        jnp.float32
    )
    coarse_ids = jnp.arange(ncoarse, dtype=jnp.float32)[None, :]
    own = corners.astype(jnp.float32)
    parts = [coupling_mat[:, f * size : (f + 1) * size].T for f in range(4)]
    tagged = [jnp.concatenate([part, jnp.broadcast_to(own, (8, ncl))], axis=0) for part in parts]
    pick = (own[:, None] == coarse_ids).astype(jnp.float32)
    columns = []
    for f, got in enumerate(facing(tagged)):
        their_pick = (got[size][:, None] == coarse_ids).astype(jnp.float32)
        theirs = jnp.dot(match[f], got[:size], precision=HIGHEST)
        columns.append(
            jnp.dot(parts[f], pick, precision=HIGHEST)
            - jnp.dot(theirs, their_pick, precision=HIGHEST)
        )
    coupling_jump = jnp.concatenate(columns, axis=0)

    def reduced(local_load, *rows):
        rows = list(rows) + [jnp.zeros_like(rows[0])] * (3 - len(rows))
        block = jnp.concatenate([local_load] + [row[None] for row in rows], axis=0)
        total = lax.psum(jnp.dot(place, block, precision=HIGHEST), ("sx", "sy"))
        return (total[:ncoarse], total[ncoarse + 1], total[ncoarse + 2], total[ncoarse + 3])

    def coarse(rhs):
        sol = jnp.dot(inverse, rhs, precision=HIGHEST)
        return (jnp.dot(coupling_jump, sol, precision=HIGHEST), inner(rhs, sol))

    def precondition(residual):
        spread = scale * residual
        applied = jnp.dot(prec_mat, spread, precision=HIGH)
        return (0.5 * jump(applied, match), 0.5 * inner(spread, applied))

    def flexible(direction):
        spread = scale * direction
        return (
            spread,
            jnp.dot(flex_mat, spread, precision=HIGH),
            jnp.dot(coupling_mat, spread, precision=HIGH),
        )

    residual = jump(loads[0, 0], match)
    direction, dot_part = precondition(residual)
    spread, flexed, load = flexible(direction)
    rhs, res_dot, energy, _ = reduced(load, dot_part, inner(spread, flexed))
    image = jump(flexed, match)
    correction, coarse_energy = coarse(rhs)
    step = res_dot / (energy + coarse_energy)
    residual = residual - step * (image + correction)
    multipliers = step * direction
    precond, dot_part = precondition(residual)
    spread, new_flexed, load = flexible(precond)
    new_rhs, new_dot, new_energy, cross = reduced(
        load, dot_part, inner(spread, new_flexed), inner(spread, flexed)
    )
    new_image = jump(new_flexed, match)
    beta = new_dot / res_dot
    rhs = new_rhs + beta * rhs
    energy = new_energy + beta * (2.0 * cross + beta * energy)
    correction, coarse_energy = coarse(rhs)
    step = new_dot / (energy + coarse_energy)
    multipliers = multipliers + step * (precond + beta * direction)
    residual = residual - step * (new_image + beta * image + correction)
    return (multipliers[None, None], residual[None, None])


def solution(mesh):
    return jax.shard_map(
        shards,
        mesh=mesh,
        in_specs=(
            P("sx", "sy", None, None),
            P("sx", "sy", None, None),
            P("sx", "sy", None, None),
            P("sx", "sy", None, None),
            P("sx", "sy", None),
            P("sx", "sy", None, None),
            P(("sx", "sy"), None),
        ),
        out_specs=(P("sx", "sy", None, None), P("sx", "sy", None, None)),
        check_vma=False,
    )
```

profile of v0, /device:TPU:1, one launch (start us, length us, event | category | flops | bytes accessed | tf_op | source)
XLA Modules:
  0.0 480.3 jit_solution(9736556489605518894)
XLA Ops:
  9.5 4.6 collective-permute-start.12
  14.1 1.9 collective-permute-start.13
  16.0 3.5 collective-permute-start.14
  21.0 2.5 slice_bitcast_fusion.6
  23.5 3.9 collective-permute-start
  31.2 1.9 collective-permute-start.1
  33.7 2.7 convolution_subtract_fusion
  36.4 4.3 collective-permute-start.2
  42.6 1.9 collective-permute-start.3
  49.7 5.8 %collective-permute-done.3 = f32[384,256]{1,0:T(8,128)S(1)} collective-permute-done((f32[384,256]{1,0:T(8,128)S(1)}, f32[384,256]{1,0:T(8,128)S(1)}, u32[]{:S(2)}, u32[]{:S(2)}) %collective-permute-start.3) | collective-permute-done | bytes 393248 | tf_op jit(solution)/shard_map/ppermute | solution.py:13
  56.1 4.1 multiply_reduce_fusion.4
  60.4 4.6 collective-permute-start.4
  66.4 3.4 collective-permute-start.6
  71.1 2.5 collective-permute-start.5
  74.2 4.1 collective-permute-done.6
  78.8 3.3 collective-permute-done.7
  83.3 4.2 multiply_reduce_fusion.3
  88.4 4.1 collective-permute-start.8
  92.5 5.6 %collective-permute-start.10 = (f32[384,256]{1,0:T(8,128)}, f32[384,256]{1,0:T(8,128)}, u32[]{:S(2)}, u32[]{:S(2)}) collective-permute-start(f32[384,256]{1,0:T(8,128)} %get-tuple-element.13), channel_id=1, source_target_pairs={{0,1},{1,2},{2,3},{3,4},{4,5},{5,6},{6,7},{7,8},{8,9},{9,10},{10,1... | collective-permute-start | bytes 1179656 | tf_op jit(solution)/shard_map/ppermute | solution.py:13
  99.4 1.9 collective-permute-start.9
  103.5 2.3 convolution_subtract_fusion.15
  106.0 2.3 convolution_subtract_fusion.13
  108.3 2.3 collective-permute-done.11
  110.7 2.3 convolution_subtract_fusion.12
  113.0 2.3 convolution_subtract_fusion.14
  115.3 1.6 reshape.275
  116.8 134.1 %all-reduce.3.cloned.1.call-done = f32[520,256]{1,0:T(8,128)} async-done(((f32[520,256]{1,0:T(8,128)}), f32[520,256]{1,0:T(8,128)}) %all-reduce.3.cloned.1.call-update) | async-done | bytes 532496 | tf_op jit(solution)/shard_map/psum | solution.py:77
  251.0 3.7 fusion.36
  254.7 2.0 copy.28
  258.8 5.7 %fusion.9 = f32[1536,256]{1,0:T(8,128)S(1)} fusion(f32[256,512]{1,0:T(8,128)} %fusion.36, f32[384,512]{1,0:T(8,128)} %convolution_subtract_fusion, f32[384,512]{1,0:T(8,128)} %convolution_subtract_fusion.1, f32[384,512]{1,0:T(8,128)} %convolution_subtract_fusion.2, f32[384,512]{1,0:T(8,128)} %convolution_subtract_fusion.3, ...), kind=kOutput, calls=%fused_computation.11 | convolution fusion | flops 2421817344 | bytes 8389632 | tf_op jit(solution)/shard_map/dot_general | solution.py:82
  264.6 7.4 %multiply_reduce_fusion.2 = (f32[256]{0:T(256)S(1)}, f32[1536,256]{1,0:T(8,128)S(1)}) fusion(f32[1536,256]{1,0:T(8,128)S(1)} %fusion.9, f32[1536]{0:T(1024)S(1)} %mul.194, f32[1,1,1536,1536]{3,2,1,0:T(8,128)} %param.9), kind=kOutput, calls=%fused_computation.34 | convolution fusion | flops 3625451264 | bytes 12590080 | tf_op jit(solution)/shard_map/dot_general | solution.py:86
  272.2 3.2 collective-permute-start.16
  275.3 1.9 collective-permute-start.18
  278.6 2.5 collective-permute-start.17
  281.6 4.1 collective-permute-done.18
  286.2 3.3 collective-permute-done.19
  290.7 5.8 %multiply_reduce_fusion.1 = (f32[256]{0:T(256)S(1)}, f32[256]{0:T(256)S(1)}, f32[1536,256]{1,0:T(8,128)}) fusion(f32[1536]{0:T(1024)S(1)} %broadcast_multiply_fusion, f32[384,256]{1,0:T(8,128)S(1)} %convolution_subtract_fusion.8, f32[384,256]{1,0:T(8,128)S(1)} %convolution_subtract_fusion.9, f32[384,256]{1,0:T(8,128)S(1)} %convolution_subtract_fusion.10, ...), kind=kOutput, calls=%fused_computation.33 | convolution fusion | flops 3628596736 | bytes 14163968 | tf_op jit(solution)/shard_map/dot_general | solution.py:93
  299.5 3.8 collective-permute-start.20
  303.3 3.9 collective-permute-start.22
  308.4 2.2 collective-permute-start.21
  310.6 139.0 %all-reduce.5.cloned.1.call-done = f32[520,256]{1,0:T(8,128)} async-done(((f32[520,256]{1,0:T(8,128)}), f32[520,256]{1,0:T(8,128)}) %all-reduce.5.cloned.1.call-update) | async-done | bytes 532496 | tf_op jit(solution)/shard_map/psum | solution.py:77
  450.4 3.9 fusion.40
  454.2 2.1 copy.31
  458.9 2.7 fusion.25
  461.6 1.7 convolution_subtract_fusion.7
  463.3 1.7 convolution_subtract_fusion.5
  465.0 1.7 convolution_subtract_fusion.4
  468.3 5.2 %fusion.29 = f32[1,1,1536,256]{3,2,1,0:T(8,128)} fusion(f32[1536,256]{1,0:T(8,128)S(1)} %copy-done.23, f32[384,256]{1,0:T(8,128)S(1)} %convolution_subtract_fusion.4, f32[384,256]{1,0:T(8,128)S(1)} %convolution_subtract_fusion.5, f32[384,256]{1,0:T(8,128)S(1)} %convolution_subtract_fusion.6, f32[384,256]{1,0:T(8,128)S(1)} %convolution_subtract_fusion.7, ...), kind=kOutput, calls=%fused_computation.31 | convolution fusion | flops 2422603776 | bytes 9963520 | tf_op jit(solution)/shard_map/dot_general | solution.py:82
  (173 shorter events, 39.8 us)
Async XLA Ops:
  7.2 108.1 %all-gather.3.cloned.1.call-start = ((), (), s32[]{:S(2)}) async-start(), calls=%async_computation.2 | async-start | bytes 1056768 | tf_op jit(solution)/shard_map/all_gather | solution.py:54
  7.9 243.1 %all-reduce.3.cloned.1.call-start = ((), (), s32[]{:S(2)}) async-start(), calls=%async_computation | async-start | bytes 1064960 | tf_op jit(solution)/shard_map/psum | solution.py:77
  9.5 36.9 %collective-permute-start.12 = (f32[392,16]{0,1:T(8,128)S(1)}, f32[392,16]{0,1:T(8,128)S(1)}, u32[]{:S(2)}, u32[]{:S(2)}) collective-permute-start(f32[392,16]{0,1:T(8,128)S(1)} %get-tuple-element.28), channel_id=1, source_target_pairs={{0,16},{16,32},{32,48},{48,64},{64,80},{80,96},{96,112},{1,17},{17... | collective-permute-start | bytes 75272 | tf_op jit(solution)/shard_map/ppermute | solution.py:13
  14.1 28.5 %collective-permute-start.13 = (f32[392,16]{0,1:T(8,128)S(1)}, f32[392,16]{0,1:T(8,128)S(1)}, u32[]{:S(2)}, u32[]{:S(2)}) collective-permute-start(f32[392,16]{0,1:T(8,128)S(1)} %get-tuple-element.29), channel_id=1, source_target_pairs={{16,0},{32,16},{48,32},{64,48},{80,64},{96,80},{112,96},{17,1},{33... | collective-permute-start | bytes 75272 | tf_op jit(solution)/shard_map/ppermute | solution.py:13
  16.0 20.4 %collective-permute-start.14 = (f32[392,16]{0,1:T(8,128)S(1)}, f32[392,16]{0,1:T(8,128)S(1)}, u32[]{:S(2)}, u32[]{:S(2)}) collective-permute-start(f32[392,16]{0,1:T(8,128)S(1)} %get-tuple-element.30), channel_id=1, source_target_pairs={{0,1},{1,2},{2,3},{3,4},{4,5},{5,6},{6,7},{7,8},{8,9},{9,10},{10,1... | collective-permute-start | bytes 75272 | tf_op jit(solution)/shard_map/ppermute | solution.py:13
  19.6 11.7 %collective-permute-start.15 = (f32[392,16]{0,1:T(8,128)S(1)}, f32[392,16]{0,1:T(8,128)S(1)}, u32[]{:S(2)}, u32[]{:S(2)}) collective-permute-start(f32[392,16]{0,1:T(8,128)S(1)} %get-tuple-element.31), channel_id=1, source_target_pairs={{1,0},{2,1},{3,2},{4,3},{5,4},{6,5},{7,6},{8,7},{9,8},{10,9},{11,1... | collective-permute-start | bytes 75272 | tf_op jit(solution)/shard_map/ppermute | solution.py:13
  23.5 23.4 %collective-permute-start = (f32[384,256]{1,0:T(8,128)}, f32[384,256]{1,0:T(8,128)}, u32[]{:S(2)}, u32[]{:S(2)}) collective-permute-start(f32[384,256]{1,0:T(8,128)} %get-tuple-element.20), channel_id=1, source_target_pairs={{0,16},{16,32},{32,48},{48,64},{64,80},{80,96},{96,112},{1,17},{17... | collective-permute-start | bytes 1179656 | tf_op jit(solution)/shard_map/ppermute | solution.py:13
  31.2 17.3 %collective-permute-start.1 = (f32[384,256]{1,0:T(8,128)}, f32[384,256]{1,0:T(8,128)S(1)}, u32[]{:S(2)}, u32[]{:S(2)}) collective-permute-start(f32[384,256]{1,0:T(8,128)} %get-tuple-element.21), channel_id=1, source_target_pairs={{16,0},{32,16},{48,32},{64,48},{80,64},{96,80},{112,96},{17,1},{33... | collective-permute-start | bytes 1179656 | tf_op jit(solution)/shard_map/ppermute | solution.py:13
  33.7 8.9 %copy-start.29 = (f32[384,256]{1,0:T(8,128)S(1)}, f32[384,256]{1,0:T(8,128)}, u32[]{:S(2)}) copy-start(f32[384,256]{1,0:T(8,128)} %get-tuple-element.23) | copy-start | bytes 1179652
  33.7 13.3 %copy-start.10 = (f32[1,1,1536,256]{3,2,1,0:T(8,128)S(1)}, f32[1,1,1536,256]{3,2,1,0:T(8,128)}, u32[]{:S(2)}) copy-start(f32[1,1,1536,256]{3,2,1,0:T(8,128)} %param.7) | copy-start | bytes 4718596
  36.4 12.7 %collective-permute-start.2 = (f32[384,256]{1,0:T(8,128)}, f32[384,256]{1,0:T(8,128)S(1)}, u32[]{:S(2)}, u32[]{:S(2)}) collective-permute-start(f32[384,256]{1,0:T(8,128)} %get-tuple-element.22), channel_id=1, source_target_pairs={{0,1},{1,2},{2,3},{3,4},{4,5},{5,6},{6,7},{7,8},{8,9},{9,10},{10,1... | collective-permute-start | bytes 1179656 | tf_op jit(solution)/shard_map/ppermute | solution.py:13
  40.8 15.3 %copy-start = (f32[1,1,1536,1536]{3,2,1,0:T(8,128)S(1)}, f32[1,1,1536,1536]{3,2,1,0:T(8,128)}, u32[]{:S(2)}) copy-start(f32[1,1,1536,1536]{3,2,1,0:T(8,128)} %param.9) | copy-start | bytes 28311556
  42.6 12.9 %collective-permute-start.3 = (f32[384,256]{1,0:T(8,128)S(1)}, f32[384,256]{1,0:T(8,128)S(1)}, u32[]{:S(2)}, u32[]{:S(2)}) collective-permute-start(f32[384,256]{1,0:T(8,128)S(1)} %copy-done.29), channel_id=1, source_target_pairs={{1,0},{2,1},{3,2},{4,3},{5,4},{6,5},{7,6},{8,7},{9,8},{10,9},{11,1... | collective-permute-start | bytes 1179656 | tf_op jit(solution)/shard_map/ppermute | solution.py:13
  49.1 11.1 %copy-start.18 = (f32[384,256]{1,0:T(8,128)}, f32[384,256]{1,0:T(8,128)S(1)}, u32[]{:S(2)}) copy-start(f32[384,256]{1,0:T(8,128)S(1)} %convolution_subtract_fusion.22) | copy-start | bytes 1179652
  49.7 10.6 %copy-start.19 = (f32[384,256]{1,0:T(8,128)}, f32[384,256]{1,0:T(8,128)S(1)}, u32[]{:S(2)}) copy-start(f32[384,256]{1,0:T(8,128)S(1)} %convolution_subtract_fusion.21) | copy-start | bytes 1179652
  56.1 27.2 %slice-start = ((s8[9437184]{0:T(1024)(128)(4,1)}), s8[4194304]{0:T(1024)(128)(4,1)S(1)}, s32[]{:S(2)}) async-start(s8[9437184]{0:T(1024)(128)(4,1)} %bitcast.172), calls=%async_computation.3 | async-start | bytes 8388608
  56.1 27.2 %slice-start.1 = ((s8[9437184]{0:T(1024)(128)(4,1)}), s8[1048576]{0:T(1024)(128)(4,1)S(1)}, s32[]{:S(2)}) async-start(s8[9437184]{0:T(1024)(128)(4,1)} %bitcast.172), calls=%async_computation.4 | async-start | bytes 2097152
  60.3 23.0 %slice-start.2 = ((s8[9437184]{0:T(1024)(128)(4,1)}), s8[4194304]{0:T(1024)(128)(4,1)S(1)}, s32[]{:S(2)}) async-start(s8[9437184]{0:T(1024)(128)(4,1)} %bitcast.172), calls=%async_computation.5 | async-start | bytes 8388608
  60.4 13.2 %collective-permute-start.4 = (f32[384,256]{1,0:T(8,128)S(1)}, f32[384,256]{1,0:T(8,128)S(1)}, u32[]{:S(2)}, u32[]{:S(2)}) collective-permute-start(f32[384,256]{1,0:T(8,128)S(1)} %get-tuple-element.16), channel_id=1, source_target_pairs={{0,16},{16,32},{32,48},{48,64},{64,80},{80,96},{96,112},{1,17},{17... | collective-permute-start | bytes 1179656 | tf_op jit(solution)/shard_map/ppermute | solution.py:13
  66.4 11.9 %collective-permute-start.6 = (f32[384,256]{1,0:T(8,128)S(1)}, f32[384,256]{1,0:T(8,128)S(1)}, u32[]{:S(2)}, u32[]{:S(2)}) collective-permute-start(f32[384,256]{1,0:T(8,128)S(1)} %get-tuple-element.17), channel_id=1, source_target_pairs={{0,1},{1,2},{2,3},{3,4},{4,5},{5,6},{6,7},{7,8},{8,9},{9,10},{10,1... | collective-permute-start | bytes 1179656 | tf_op jit(solution)/shard_map/ppermute | solution.py:13
  69.8 12.4 %collective-permute-start.7 = (f32[384,256]{1,0:T(8,128)S(1)}, f32[384,256]{1,0:T(8,128)S(1)}, u32[]{:S(2)}, u32[]{:S(2)}) collective-permute-start(f32[384,256]{1,0:T(8,128)S(1)} %get-tuple-element.18), channel_id=1, source_target_pairs={{1,0},{2,1},{3,2},{4,3},{5,4},{6,5},{7,6},{8,7},{9,8},{10,9},{11,1... | collective-permute-start | bytes 1179656 | tf_op jit(solution)/shard_map/ppermute | solution.py:13
  71.1 11.6 %collective-permute-start.5 = (f32[384,256]{1,0:T(8,128)S(1)}, f32[384,256]{1,0:T(8,128)S(1)}, u32[]{:S(2)}, u32[]{:S(2)}) collective-permute-start(f32[384,256]{1,0:T(8,128)S(1)} %get-tuple-element.19), channel_id=1, source_target_pairs={{16,0},{32,16},{48,32},{64,48},{80,64},{96,80},{112,96},{17,1},{33... | collective-permute-start | bytes 1179656 | tf_op jit(solution)/shard_map/ppermute | solution.py:13
  74.1 27.2 %copy-start.2 = (f32[384,256]{1,0:T(8,128)}, f32[384,256]{1,0:T(8,128)S(1)}, u32[]{:S(2)}) copy-start(f32[384,256]{1,0:T(8,128)S(1)} %convolution_subtract_fusion.19) | copy-start | bytes 1179652
  78.8 22.5 %copy-start.4 = (f32[384,256]{1,0:T(8,128)}, f32[384,256]{1,0:T(8,128)S(1)}, u32[]{:S(2)}) copy-start(f32[384,256]{1,0:T(8,128)S(1)} %convolution_subtract_fusion.17) | copy-start | bytes 1179652
  82.7 18.7 %copy-start.6 = (f32[384,256]{1,0:T(8,128)}, f32[384,256]{1,0:T(8,128)S(1)}, u32[]{:S(2)}) copy-start(f32[384,256]{1,0:T(8,128)S(1)} %convolution_subtract_fusion.16) | copy-start | bytes 1179652
  83.3 18.1 %copy-start.8 = (f32[384,256]{1,0:T(8,128)}, f32[384,256]{1,0:T(8,128)S(1)}, u32[]{:S(2)}) copy-start(f32[384,256]{1,0:T(8,128)S(1)} %convolution_subtract_fusion.18) | copy-start | bytes 1179652
  88.4 15.0 %collective-permute-start.8 = (f32[384,256]{1,0:T(8,128)}, f32[384,256]{1,0:T(8,128)}, u32[]{:S(2)}, u32[]{:S(2)}) collective-permute-start(f32[384,256]{1,0:T(8,128)} %get-tuple-element.12), channel_id=1, source_target_pairs={{0,16},{16,32},{32,48},{48,64},{64,80},{80,96},{96,112},{1,17},{17... | collective-permute-start | bytes 1179656 | tf_op jit(solution)/shard_map/ppermute | solution.py:13
  92.5 13.6 %collective-permute-start.10 = (f32[384,256]{1,0:T(8,128)}, f32[384,256]{1,0:T(8,128)}, u32[]{:S(2)}, u32[]{:S(2)}) collective-permute-start(f32[384,256]{1,0:T(8,128)} %get-tuple-element.13), channel_id=1, source_target_pairs={{0,1},{1,2},{2,3},{3,4},{4,5},{5,6},{6,7},{7,8},{8,9},{9,10},{10,1... | collective-permute-start | bytes 1179656 | tf_op jit(solution)/shard_map/ppermute | solution.py:13
  98.1 12.5 %collective-permute-start.11 = (f32[384,256]{1,0:T(8,128)S(1)}, f32[384,256]{1,0:T(8,128)}, u32[]{:S(2)}, u32[]{:S(2)}) collective-permute-start(f32[384,256]{1,0:T(8,128)S(1)} %get-tuple-element.14), channel_id=1, source_target_pairs={{1,0},{2,1},{3,2},{4,3},{5,4},{6,5},{7,6},{8,7},{9,8},{10,9},{11,1... | collective-permute-start | bytes 1179656 | tf_op jit(solution)/shard_map/ppermute | solution.py:13
  99.4 13.6 %collective-permute-start.9 = (f32[384,256]{1,0:T(8,128)S(1)}, f32[384,256]{1,0:T(8,128)}, u32[]{:S(2)}, u32[]{:S(2)}) collective-permute-start(f32[384,256]{1,0:T(8,128)S(1)} %get-tuple-element.15), channel_id=1, source_target_pairs={{16,0},{32,16},{48,32},{64,48},{80,64},{96,80},{112,96},{17,1},{33... | collective-permute-start | bytes 1179656 | tf_op jit(solution)/shard_map/ppermute | solution.py:13
  103.2 346.4 %all-reduce.5.cloned.1.call-start = ((), (), s32[]{:S(2)}) async-start(), calls=%async_computation.1 | async-start | bytes 1064960 | tf_op jit(solution)/shard_map/psum | solution.py:77
  264.5 26.1 %slice-start.3 = ((s8[9437184]{0:T(1024)(128)(4,1)}), s8[4194304]{0:T(1024)(128)(4,1)S(1)}, s32[]{:S(2)}) async-start(s8[9437184]{0:T(1024)(128)(4,1)} %bitcast.174), calls=%async_computation.6 | async-start | bytes 8388608
  264.6 26.1 %slice-start.4 = ((s8[9437184]{0:T(1024)(128)(4,1)}), s8[4194304]{0:T(1024)(128)(4,1)S(1)}, s32[]{:S(2)}) async-start(s8[9437184]{0:T(1024)(128)(4,1)} %bitcast.174), calls=%async_computation.7 | async-start | bytes 8388608
  272.0 18.6 %slice-start.5 = ((s8[9437184]{0:T(1024)(128)(4,1)}), s8[1048576]{0:T(1024)(128)(4,1)S(1)}, s32[]{:S(2)}) async-start(s8[9437184]{0:T(1024)(128)(4,1)} %bitcast.174), calls=%async_computation.8 | async-start | bytes 2097152
  272.2 8.9 %collective-permute-start.16 = (f32[384,256]{1,0:T(8,128)S(1)}, f32[384,256]{1,0:T(8,128)S(1)}, u32[]{:S(2)}, u32[]{:S(2)}) collective-permute-start(f32[384,256]{1,0:T(8,128)S(1)} %get-tuple-element.8), channel_id=1, source_target_pairs={{0,16},{16,32},{32,48},{48,64},{64,80},{80,96},{96,112},{1,17},{17... | collective-permute-start | bytes 1179656 | tf_op jit(solution)/shard_map/ppermute | solution.py:13
  275.3 10.4 %collective-permute-start.18 = (f32[384,256]{1,0:T(8,128)S(1)}, f32[384,256]{1,0:T(8,128)S(1)}, u32[]{:S(2)}, u32[]{:S(2)}) collective-permute-start(f32[384,256]{1,0:T(8,128)S(1)} %get-tuple-element.9), channel_id=1, source_target_pairs={{0,1},{1,2},{2,3},{3,4},{4,5},{5,6},{6,7},{7,8},{8,9},{9,10},{10,1... | collective-permute-start | bytes 1179656 | tf_op jit(solution)/shard_map/ppermute | solution.py:13
  277.3 12.2 %collective-permute-start.19 = (f32[384,256]{1,0:T(8,128)S(1)}, f32[384,256]{1,0:T(8,128)S(1)}, u32[]{:S(2)}, u32[]{:S(2)}) collective-permute-start(f32[384,256]{1,0:T(8,128)S(1)} %get-tuple-element.10), channel_id=1, source_target_pairs={{1,0},{2,1},{3,2},{4,3},{5,4},{6,5},{7,6},{8,7},{9,8},{10,9},{11,1... | collective-permute-start | bytes 1179656 | tf_op jit(solution)/shard_map/ppermute | solution.py:13
  278.6 11.5 %collective-permute-start.17 = (f32[384,256]{1,0:T(8,128)S(1)}, f32[384,256]{1,0:T(8,128)S(1)}, u32[]{:S(2)}, u32[]{:S(2)}) collective-permute-start(f32[384,256]{1,0:T(8,128)S(1)} %get-tuple-element.11), channel_id=1, source_target_pairs={{16,0},{32,16},{48,32},{64,48},{80,64},{96,80},{112,96},{17,1},{33... | collective-permute-start | bytes 1179656 | tf_op jit(solution)/shard_map/ppermute | solution.py:13
  281.6 14.8 %copy-start.11 = (f32[384,256]{1,0:T(8,128)}, f32[384,256]{1,0:T(8,128)S(1)}, u32[]{:S(2)}) copy-start(f32[384,256]{1,0:T(8,128)S(1)} %convolution_subtract_fusion.11) | copy-start | bytes 1179652
  286.2 10.2 %copy-start.13 = (f32[384,256]{1,0:T(8,128)}, f32[384,256]{1,0:T(8,128)S(1)}, u32[]{:S(2)}) copy-start(f32[384,256]{1,0:T(8,128)S(1)} %convolution_subtract_fusion.9) | copy-start | bytes 1179652
  299.5 162.1 %collective-permute-start.20 = (f32[384,256]{1,0:T(8,128)}, f32[384,256]{1,0:T(8,128)}, u32[]{:S(2)}, u32[]{:S(2)}) collective-permute-start(f32[384,256]{1,0:T(8,128)} %get-tuple-element.4), channel_id=1, source_target_pairs={{0,16},{16,32},{32,48},{48,64},{64,80},{80,96},{96,112},{1,17},{17... | collective-permute-start | bytes 1179656 | tf_op jit(solution)/shard_map/ppermute | solution.py:13
  303.3 160.0 %collective-permute-start.22 = (f32[384,256]{1,0:T(8,128)}, f32[384,256]{1,0:T(8,128)}, u32[]{:S(2)}, u32[]{:S(2)}) collective-permute-start(f32[384,256]{1,0:T(8,128)} %get-tuple-element.5), channel_id=1, source_target_pairs={{0,1},{1,2},{2,3},{3,4},{4,5},{5,6},{6,7},{7,8},{8,9},{9,10},{10,1... | collective-permute-start | bytes 1179656 | tf_op jit(solution)/shard_map/ppermute | solution.py:13
  307.2 157.8 %collective-permute-start.23 = (f32[384,256]{1,0:T(8,128)}, f32[384,256]{1,0:T(8,128)}, u32[]{:S(2)}, u32[]{:S(2)}) collective-permute-start(f32[384,256]{1,0:T(8,128)} %get-tuple-element.6), channel_id=1, source_target_pairs={{1,0},{2,1},{3,2},{4,3},{5,4},{6,5},{7,6},{8,7},{9,8},{10,9},{11,1... | collective-permute-start | bytes 1179656 | tf_op jit(solution)/shard_map/ppermute | solution.py:13
  308.4 158.2 %collective-permute-start.21 = (f32[384,256]{1,0:T(8,128)}, f32[384,256]{1,0:T(8,128)}, u32[]{:S(2)}, u32[]{:S(2)}) collective-permute-start(f32[384,256]{1,0:T(8,128)} %get-tuple-element.7), channel_id=1, source_target_pairs={{16,0},{32,16},{48,32},{64,48},{80,64},{96,80},{112,96},{17,1},{33... | collective-permute-start | bytes 1179656 | tf_op jit(solution)/shard_map/ppermute | solution.py:13
  458.8 9.4 %copy-start.30 = (f32[384,256]{1,0:T(8,128)S(1)}, f32[384,256]{1,0:T(8,128)}, u32[]{:S(2)}) copy-start(f32[384,256]{1,0:T(8,128)} %convolution_subtract_fusion.15) | copy-start | bytes 1179652
  458.8 9.4 %copy-start.31 = (f32[384,256]{1,0:T(8,128)S(1)}, f32[384,256]{1,0:T(8,128)}, u32[]{:S(2)}) copy-start(f32[384,256]{1,0:T(8,128)} %convolution_subtract_fusion.13) | copy-start | bytes 1179652
  458.9 9.4 %copy-start.32 = (f32[384,256]{1,0:T(8,128)S(1)}, f32[384,256]{1,0:T(8,128)}, u32[]{:S(2)}) copy-start(f32[384,256]{1,0:T(8,128)} %convolution_subtract_fusion.12) | copy-start | bytes 1179652
  458.9 9.4 %copy-start.33 = (f32[384,256]{1,0:T(8,128)S(1)}, f32[384,256]{1,0:T(8,128)}, u32[]{:S(2)}) copy-start(f32[384,256]{1,0:T(8,128)} %convolution_subtract_fusion.14) | copy-start | bytes 1179652
  (21 other events, 97.6 us)
Sparse Core Ops, SparseCore 0:
  10.8 72.5 all-gather.2
  103.3 147.5 all-reduce.2
  298.4 151.1 all-reduce.4
where the time goes:
time: 486 us; the launch traced here: 480 us
  waiting for transfers between devices  297 us (61%)
  matrix products  78.2 us (16%)
  starting transfers between devices  68.4 us (14%)
  between operations  15.1 us (3%)
  local copies, waits for them, and re-layouts  12.4 us (3%)
  other arithmetic  9.11 us (2%)
    psum x2, waiting for transfers between devices, reduced(): total = lax.psum(jnp.dot(place, block, precision=HIGHEST), ('sx', 'sy'))  273 us
    ppermute x24, starting transfers between devices, shifted(): return lax.ppermute(block, axis, route)  68.1 us
    ppermute x24, waiting for transfers between devices, shifted(): return lax.ppermute(block, axis, route)  23.2 us
    dot_general x20, matrix products, jump(): jnp.dot(match[f], received[f], precision=HIGHEST)  23.1 us
    dot_general x2, matrix products, precondition(): applied = jnp.dot(prec_mat, spread, precision=HIGH)  11.6 us
    dot_general x2, matrix products, coarse(): return (jnp.dot(coupling_jump, sol, precision=HIGHEST), inner(rhs, sol))  10.9 us
    dot_general x2, matrix products, flexible(): jnp.dot(flex_mat, spread, precision=HIGH)  9.93 us
  transfers between devices with their start and end apart: 27, of which 9 were waited for; matrix products, arithmetic and copies ran while one was open for 13% of the time, Pallas kernels for 0%

commit v1 on v0

--- a/solution.py
+++ b/solution.py
@@ -74,7 +74,7 @@
     def reduced(local_load, *rows):
         rows = list(rows) + [jnp.zeros_like(rows[0])] * (3 - len(rows))
         block = jnp.concatenate([local_load] + [row[None] for row in rows], axis=0)
-        total = lax.psum(jnp.dot(place, block, precision=HIGHEST), ("sx", "sy"))
+        total = lax.psum(lax.psum(jnp.dot(place, block, precision=HIGHEST), "sx"), "sy")
         return (total[:ncoarse], total[ncoarse + 1], total[ncoarse + 2], total[ncoarse + 3])
 
     def coarse(rhs):

time: 486 us -> 452 us (0.930)
  waiting for transfers between devices: 297 us -> 257 us
  matrix products: 78.2 us -> 85.5 us
    psum x2 -> x4, waiting for transfers between devices: 273 us -> 228 us  [the longest x2 149 us: reduced(): lax.psum(lax.psum(jnp.dot(place, block, precision=HIGHEST), 'sx'), 'sy')]
    all_gather x1, waiting for transfers between devices: 0.01 us -> 7.75 us  [shards(): inverse = lax.all_gather(coarse_inverse, ('sx', 'sy'), axis=0, tiled=True)]
    dot_general x20, matrix products: 23.1 us -> 29 us  [jump(): jnp.dot(match[f], received[f], precision=HIGHEST)]
  transfers between devices with their start and end apart: 27 -> 29, of which waited for: 9 -> 12; matrix products, arithmetic and copies ran while one was open for 13% -> 9% of each run, Pallas kernels for 0% -> 0%
where the time goes in v1:
time: 452 us; the launch traced here: 444 us
  waiting for transfers between devices  257 us (57%)
  matrix products  85.5 us (19%)
  starting transfers between devices  68.1 us (15%)
  between operations  16.6 us (4%)
  local copies, waits for them, and re-layouts  9.63 us (2%)
  other arithmetic  6.94 us (2%)
    psum x2, waiting for transfers between devices, reduced(): lax.psum(lax.psum(jnp.dot(place, block, precision=HIGHEST), 'sx'), 'sy')  149 us
    psum x2, waiting for transfers between devices, reduced(): lax.psum(jnp.dot(place, block, precision=HIGHEST), 'sx')  78.6 us
    ppermute x24, starting transfers between devices, shifted(): return lax.ppermute(block, axis, route)  67.9 us
    dot_general x20, matrix products, jump(): jnp.dot(match[f], received[f], precision=HIGHEST)  29 us
    ppermute x24, waiting for transfers between devices, shifted(): return lax.ppermute(block, axis, route)  21.5 us
    dot_general x2, matrix products, precondition(): applied = jnp.dot(prec_mat, spread, precision=HIGH)  15.4 us
    dot_general x2, matrix products, coarse(): return (jnp.dot(coupling_jump, sol, precision=HIGHEST), inner(rhs, sol))  12.3 us
  transfers between devices with their start and end apart: 29, of which 12 were waited for; matrix products, arithmetic and copies ran while one was open for 9% of the time, Pallas kernels for 0%

profile of v1, /device:TPU:1, one launch (start us, length us, event | category | flops | bytes accessed | tf_op | source)
XLA Modules:
  0.0 443.7 jit_solution(15542945541701174909)
XLA Ops:
  8.1 2.5 slice_bitcast_fusion.6
  10.6 4.6 %collective-permute-start = (f32[384,256]{1,0:T(8,128)}, f32[384,256]{1,0:T(8,128)}, u32[]{:S(2)}, u32[]{:S(2)}) collective-permute-start(f32[384,256]{1,0:T(8,128)} %get-tuple-element.20), channel_id=1, source_target_pairs={{0,16},{16,32},{32,48},{48,64},{64,80},{80,96},{96,112},{1,17},{17... | collective-permute-start | bytes 1179656 | tf_op jit(solution)/shard_map/ppermute | solution.py:13
  15.2 1.9 collective-permute-start.1
  17.1 4.3 collective-permute-start.2
  26.7 2.1 collective-permute-done.2
  30.4 3.4 collective-permute-done.3
  35.4 8.0 %multiply_reduce_fusion.4 = (f32[256]{0:T(256)S(1)}, f32[1536,256]{1,0:T(8,128)S(1)}) fusion(f32[1536]{0:T(1024)S(1)} %mul.194, f32[384,256]{1,0:T(8,128)S(1)} %convolution_subtract_fusion.20, f32[384,256]{1,0:T(8,128)S(1)} %convolution_subtract_fusion.21, f32[384,256]{1,0:T(8,128)S(1)} %convolution_subtract_fusion.22, ...), kind=kOutput, calls=%fused_computation.36 | convolution fusion | flops 3627810560 | bytes 12590080 | tf_op jit(solution)/shard_map/dot_general | solution.py:86
  43.5 4.4 collective-permute-start.4
  47.9 2.8 collective-permute-start.6
  52.0 2.4 collective-permute-start.5
  55.1 3.2 collective-permute-done.6
  58.8 3.6 collective-permute-done.7
  64.2 4.1 multiply_reduce_fusion.3
  69.7 4.3 collective-permute-start.12
  74.0 1.9 collective-permute-start.13
  76.0 3.4 collective-permute-start.14
  82.9 2.0 collective-permute-done.15
  91.7 4.4 %collective-permute-start.8 = (f32[384,256]{1,0:T(8,128)}, f32[384,256]{1,0:T(8,128)}, u32[]{:S(2)}, u32[]{:S(2)}) collective-permute-start(f32[384,256]{1,0:T(8,128)} %get-tuple-element.12), channel_id=1, source_target_pairs={{0,16},{16,32},{32,48},{48,64},{64,80},{80,96},{96,112},{1,17},{17... | collective-permute-start | bytes 1179656 | tf_op jit(solution)/shard_map/ppermute | solution.py:13
  96.7 4.6 %collective-permute-start.10 = (f32[384,256]{1,0:T(8,128)}, f32[384,256]{1,0:T(8,128)}, u32[]{:S(2)}, u32[]{:S(2)}) collective-permute-start(f32[384,256]{1,0:T(8,128)} %get-tuple-element.13), channel_id=1, source_target_pairs={{0,1},{1,2},{2,3},{3,4},{4,5},{5,6},{6,7},{7,8},{8,9},{9,10},{10,1... | collective-permute-start | bytes 1179656 | tf_op jit(solution)/shard_map/ppermute | solution.py:13
  104.0 1.9 collective-permute-start.9
  105.9 25.8 %all-reduce.5.cloned.1.call-done = f32[520,256]{1,0:T(8,128)} async-done(((f32[520,256]{1,0:T(8,128)}), f32[520,256]{1,0:T(8,128)}) %all-reduce.5.cloned.1.call-update) | async-done | bytes 532496 | tf_op jit(solution)/shard_map/psum | solution.py:77
  131.8 2.3 convolution_subtract_fusion.15
  134.1 2.3 convolution_subtract_fusion.13
  136.4 2.3 convolution_subtract_fusion.12
  138.7 2.3 convolution_subtract_fusion.14
  141.0 7.7 %all-gather.3.cloned.1.call-done = f32[128,4,512]{2,1,0:T(4,128)} async-done(((f32[1,4,512]{2,1,0:T(4,128)}), f32[128,4,512]{2,1,0:T(4,128)}) %all-gather.3.cloned.1.call-update) | async-done | bytes 1048592 | tf_op jit(solution)/shard_map/all_gather | solution.py:54
  150.4 69.9 %all-reduce.7.cloned.1.call-done = f32[520,256]{1,0:T(8,128)} async-done(((f32[520,256]{1,0:T(8,128)}), f32[520,256]{1,0:T(8,128)}) %all-reduce.7.cloned.1.call-update) | async-done | bytes 532496 | tf_op jit(solution)/shard_map/psum | solution.py:77
  220.2 3.7 fusion.36
  223.9 2.0 copy.28
  228.0 5.7 %fusion.9 = f32[1536,256]{1,0:T(8,128)S(1)} fusion(f32[256,512]{1,0:T(8,128)} %fusion.36, f32[384,512]{1,0:T(8,128)} %convolution_subtract_fusion, f32[384,512]{1,0:T(8,128)} %convolution_subtract_fusion.1, f32[384,512]{1,0:T(8,128)} %convolution_subtract_fusion.2, f32[384,512]{1,0:T(8,128)} %convolution_subtract_fusion.3, ...), kind=kOutput, calls=%fused_computation.11 | convolution fusion | flops 2421817344 | bytes 8389632 | tf_op jit(solution)/shard_map/dot_general | solution.py:82
  233.8 7.4 %multiply_reduce_fusion.2 = (f32[256]{0:T(256)S(1)}, f32[1536,256]{1,0:T(8,128)S(1)}) fusion(f32[1536,256]{1,0:T(8,128)S(1)} %fusion.9, f32[1536]{0:T(1024)S(1)} %mul.194, f32[1,1,1536,1536]{3,2,1,0:T(8,128)} %param.9), kind=kOutput, calls=%fused_computation.34 | convolution fusion | flops 3625451264 | bytes 12590080 | tf_op jit(solution)/shard_map/dot_general | solution.py:86
  241.4 5.2 %collective-permute-start.16 = (f32[384,256]{1,0:T(8,128)S(1)}, f32[384,256]{1,0:T(8,128)S(1)}, u32[]{:S(2)}, u32[]{:S(2)}) collective-permute-start(f32[384,256]{1,0:T(8,128)S(1)} %get-tuple-element.8), channel_id=1, source_target_pairs={{0,16},{16,32},{32,48},{48,64},{64,80},{80,96},{96,112},{1,17},{17... | collective-permute-start | bytes 1179656 | tf_op jit(solution)/shard_map/ppermute | solution.py:13
  246.7 1.9 collective-permute-start.18
  249.9 2.1 collective-permute-start.17
  252.6 3.7 collective-permute-done.18
  256.8 3.6 collective-permute-done.19
  261.5 4.8 %multiply_reduce_fusion.1 = (f32[256]{0:T(256)S(1)}, f32[256]{0:T(256)S(1)}, f32[1536,256]{1,0:T(8,128)S(1)}) fusion(f32[1536]{0:T(1024)S(1)} %broadcast_multiply_fusion, f32[384,256]{1,0:T(8,128)S(1)} %convolution_subtract_fusion.8, f32[384,256]{1,0:T(8,128)S(1)} %convolution_subtract_fusion.9, f32[384,256]{1,0:T(8,128)S(1)} %convolution_subtract_fusion.10, ...), kind=kOutput, calls=%fused_computation.33 | convolution fusion | flops 3628596736 | bytes 14163968 | tf_op jit(solution)/shard_map/dot_general | solution.py:93
  268.2 4.1 collective-permute-start.20
  273.5 3.6 collective-permute-start.22
  278.5 2.2 collective-permute-start.21
  280.7 52.8 %all-reduce.9.cloned.1.call-done = f32[520,256]{1,0:T(8,128)} async-done(((f32[520,256]{1,0:T(8,128)}), f32[520,256]{1,0:T(8,128)}) %all-reduce.9.cloned.1.call-update) | async-done | bytes 532496 | tf_op jit(solution)/shard_map/psum | solution.py:77
  333.5 2.3 convolution_subtract_fusion.7
  335.9 2.3 convolution_subtract_fusion.5
  338.2 2.3 convolution_subtract_fusion.4
  340.5 2.3 convolution_subtract_fusion.6
  342.8 79.1 %all-reduce.11.cloned.1.call-done = f32[520,256]{1,0:T(8,128)} async-done(((f32[520,256]{1,0:T(8,128)}), f32[520,256]{1,0:T(8,128)}) %all-reduce.11.cloned.1.call-update) | async-done | bytes 532496 | tf_op jit(solution)/shard_map/psum | solution.py:77
  422.6 3.1 fusion.40
  428.2 6.6 %fusion.29 = f32[1,1,1536,256]{3,2,1,0:T(8,128)} fusion(f32[1536,256]{1,0:T(8,128)S(1)} %copy-done.25, f32[384,256]{1,0:T(8,128)} %convolution_subtract_fusion.4, f32[384,256]{1,0:T(8,128)} %convolution_subtract_fusion.5, f32[384,256]{1,0:T(8,128)} %convolution_subtract_fusion.6, f32[384,256]{1,0:T(8,128)} %convolution_subtract_fusion.7, ...), kind=kOutput, calls=%fused_computation.31 | convolution fusion | flops 2422603776 | bytes 9963520 | tf_op jit(solution)/shard_map/dot_general | solution.py:82
  (167 shorter events, 43.6 us)
Async XLA Ops:
  8.0 15.5 %copy-start.11 = (f32[1,1,1536,256]{3,2,1,0:T(8,128)S(1)}, f32[1,1,1536,256]{3,2,1,0:T(8,128)}, u32[]{:S(2)}) copy-start(f32[1,1,1536,256]{3,2,1,0:T(8,128)} %param.7) | copy-start | bytes 4718596
  8.0 14.7 %copy-start.28 = (s32[1,1,4,384]{3,2,1,0:T(4,128)S(1)}, s32[1,1,4,384]{3,2,1,0:T(4,128)}, u32[]{:S(2)}) copy-start(s32[1,1,4,384]{3,2,1,0:T(4,128)} %param.12) | copy-start | bytes 18436
  8.0 15.1 %copy-start.27 = (f32[1,1,16,1536]{3,2,1,0:T(8,128)S(1)}, f32[1,1,16,1536]{3,2,1,0:T(8,128)}, u32[]{:S(2)}) copy-start(f32[1,1,16,1536]{3,2,1,0:T(8,128)} %param.10) | copy-start | bytes 294916
  8.0 15.4 %copy-start.29 = (s32[1,1,16]{2,1,0:T(1,128)S(1)}, s32[1,1,16]{2,1,0:T(1,128)}, u32[]{:S(2)}) copy-start(s32[1,1,16]{2,1,0:T(1,128)} %param.11) | copy-start | bytes 196
  8.0 123.6 %all-reduce.5.cloned.1.call-start = ((), (), s32[]{:S(2)}) async-start(), calls=%async_computation | async-start | bytes 1064960 | tf_op jit(solution)/shard_map/psum | solution.py:77
  10.6 12.9 %collective-permute-start = (f32[384,256]{1,0:T(8,128)}, f32[384,256]{1,0:T(8,128)}, u32[]{:S(2)}, u32[]{:S(2)}) collective-permute-start(f32[384,256]{1,0:T(8,128)} %get-tuple-element.20), channel_id=1, source_target_pairs={{0,16},{16,32},{32,48},{48,64},{64,80},{80,96},{96,112},{1,17},{17... | collective-permute-start | bytes 1179656 | tf_op jit(solution)/shard_map/ppermute | solution.py:13
  15.2 9.9 %collective-permute-start.1 = (f32[384,256]{1,0:T(8,128)}, f32[384,256]{1,0:T(8,128)}, u32[]{:S(2)}, u32[]{:S(2)}) collective-permute-start(f32[384,256]{1,0:T(8,128)} %get-tuple-element.21), channel_id=1, source_target_pairs={{16,0},{32,16},{48,32},{64,48},{80,64},{96,80},{112,96},{17,1},{33... | collective-permute-start | bytes 1179656 | tf_op jit(solution)/shard_map/ppermute | solution.py:13
  17.1 11.7 %collective-permute-start.2 = (f32[384,256]{1,0:T(8,128)S(1)}, f32[384,256]{1,0:T(8,128)}, u32[]{:S(2)}, u32[]{:S(2)}) collective-permute-start(f32[384,256]{1,0:T(8,128)S(1)} %get-tuple-element.22), channel_id=1, source_target_pairs={{0,1},{1,2},{2,3},{3,4},{4,5},{5,6},{6,7},{7,8},{8,9},{9,10},{10,1... | collective-permute-start | bytes 1179656 | tf_op jit(solution)/shard_map/ppermute | solution.py:13
  21.4 12.3 %collective-permute-start.3 = (f32[384,256]{1,0:T(8,128)S(1)}, f32[384,256]{1,0:T(8,128)}, u32[]{:S(2)}, u32[]{:S(2)}) collective-permute-start(f32[384,256]{1,0:T(8,128)S(1)} %get-tuple-element.23), channel_id=1, source_target_pairs={{1,0},{2,1},{3,2},{4,3},{5,4},{6,5},{7,6},{8,7},{9,8},{10,9},{11,1... | collective-permute-start | bytes 1179656 | tf_op jit(solution)/shard_map/ppermute | solution.py:13
  25.0 10.3 %copy-start.20 = (f32[384,256]{1,0:T(8,128)}, f32[384,256]{1,0:T(8,128)S(1)}, u32[]{:S(2)}) copy-start(f32[384,256]{1,0:T(8,128)S(1)} %convolution_subtract_fusion.23) | copy-start | bytes 1179652
  26.7 16.7 %copy-start.21 = (f32[384,256]{1,0:T(8,128)}, f32[384,256]{1,0:T(8,128)S(1)}, u32[]{:S(2)}) copy-start(f32[384,256]{1,0:T(8,128)S(1)} %convolution_subtract_fusion.22) | copy-start | bytes 1179652
  30.3 13.0 %copy-start.22 = (f32[384,256]{1,0:T(8,128)}, f32[384,256]{1,0:T(8,128)S(1)}, u32[]{:S(2)}) copy-start(f32[384,256]{1,0:T(8,128)S(1)} %convolution_subtract_fusion.21) | copy-start | bytes 1179652
  35.3 8.1 %copy-start.23 = (f32[384,256]{1,0:T(8,128)}, f32[384,256]{1,0:T(8,128)S(1)}, u32[]{:S(2)}) copy-start(f32[384,256]{1,0:T(8,128)S(1)} %convolution_subtract_fusion.20) | copy-start | bytes 1179652
  35.3 28.8 %slice-start = ((s8[9437184]{0:T(1024)(128)(4,1)}), s8[4194304]{0:T(1024)(128)(4,1)S(1)}, s32[]{:S(2)}) async-start(s8[9437184]{0:T(1024)(128)(4,1)} %bitcast.172), calls=%async_computation.5 | async-start | bytes 8388608
  35.3 28.8 %slice-start.1 = ((s8[9437184]{0:T(1024)(128)(4,1)}), s8[4194304]{0:T(1024)(128)(4,1)S(1)}, s32[]{:S(2)}) async-start(s8[9437184]{0:T(1024)(128)(4,1)} %bitcast.172), calls=%async_computation.6 | async-start | bytes 8388608
  43.4 20.8 %slice-start.2 = ((s8[9437184]{0:T(1024)(128)(4,1)}), s8[1048576]{0:T(1024)(128)(4,1)S(1)}, s32[]{:S(2)}) async-start(s8[9437184]{0:T(1024)(128)(4,1)} %bitcast.172), calls=%async_computation.7 | async-start | bytes 2097152
  43.5 11.0 %collective-permute-start.4 = (f32[384,256]{1,0:T(8,128)S(1)}, f32[384,256]{1,0:T(8,128)S(1)}, u32[]{:S(2)}, u32[]{:S(2)}) collective-permute-start(f32[384,256]{1,0:T(8,128)S(1)} %get-tuple-element.16), channel_id=1, source_target_pairs={{0,16},{16,32},{32,48},{48,64},{64,80},{80,96},{96,112},{1,17},{17... | collective-permute-start | bytes 1179656 | tf_op jit(solution)/shard_map/ppermute | solution.py:13
  47.9 10.3 %collective-permute-start.6 = (f32[384,256]{1,0:T(8,128)S(1)}, f32[384,256]{1,0:T(8,128)S(1)}, u32[]{:S(2)}, u32[]{:S(2)}) collective-permute-start(f32[384,256]{1,0:T(8,128)S(1)} %get-tuple-element.17), channel_id=1, source_target_pairs={{0,1},{1,2},{2,3},{3,4},{4,5},{5,6},{6,7},{7,8},{8,9},{9,10},{10,1... | collective-permute-start | bytes 1179656 | tf_op jit(solution)/shard_map/ppermute | solution.py:13
  50.7 11.7 %collective-permute-start.7 = (f32[384,256]{1,0:T(8,128)S(1)}, f32[384,256]{1,0:T(8,128)S(1)}, u32[]{:S(2)}, u32[]{:S(2)}) collective-permute-start(f32[384,256]{1,0:T(8,128)S(1)} %get-tuple-element.18), channel_id=1, source_target_pairs={{1,0},{2,1},{3,2},{4,3},{5,4},{6,5},{7,6},{8,7},{9,8},{10,9},{11,1... | collective-permute-start | bytes 1179656 | tf_op jit(solution)/shard_map/ppermute | solution.py:13
  52.0 10.9 %collective-permute-start.5 = (f32[384,256]{1,0:T(8,128)S(1)}, f32[384,256]{1,0:T(8,128)S(1)}, u32[]{:S(2)}, u32[]{:S(2)}) collective-permute-start(f32[384,256]{1,0:T(8,128)S(1)} %get-tuple-element.19), channel_id=1, source_target_pairs={{16,0},{32,16},{48,32},{64,48},{80,64},{96,80},{112,96},{17,1},{33... | collective-permute-start | bytes 1179656 | tf_op jit(solution)/shard_map/ppermute | solution.py:13
  55.0 9.1 %copy-start.3 = (f32[384,256]{1,0:T(8,128)}, f32[384,256]{1,0:T(8,128)S(1)}, u32[]{:S(2)}) copy-start(f32[384,256]{1,0:T(8,128)S(1)} %convolution_subtract_fusion.19) | copy-start | bytes 1179652
  69.6 79.2 %all-gather.3.cloned.1.call-start = ((), (), s32[]{:S(2)}) async-start(), calls=%async_computation.4 | async-start | bytes 1056768 | tf_op jit(solution)/shard_map/all_gather | solution.py:54
  69.7 26.5 %collective-permute-start.12 = (f32[392,16]{0,1:T(8,128)S(1)}, f32[392,16]{0,1:T(8,128)S(1)}, u32[]{:S(2)}, u32[]{:S(2)}) collective-permute-start(f32[392,16]{0,1:T(8,128)S(1)} %get-tuple-element.28), channel_id=1, source_target_pairs={{0,16},{16,32},{32,48},{48,64},{64,80},{80,96},{96,112},{1,17},{17... | collective-permute-start | bytes 75272 | tf_op jit(solution)/shard_map/ppermute | solution.py:13
  74.0 11.4 %collective-permute-start.13 = (f32[392,16]{0,1:T(8,128)S(1)}, f32[392,16]{0,1:T(8,128)S(1)}, u32[]{:S(2)}, u32[]{:S(2)}) collective-permute-start(f32[392,16]{0,1:T(8,128)S(1)} %get-tuple-element.29), channel_id=1, source_target_pairs={{16,0},{32,16},{48,32},{64,48},{80,64},{96,80},{112,96},{17,1},{33... | collective-permute-start | bytes 75272 | tf_op jit(solution)/shard_map/ppermute | solution.py:13
  76.0 9.6 %collective-permute-start.14 = (f32[392,16]{0,1:T(8,128)S(1)}, f32[392,16]{0,1:T(8,128)S(1)}, u32[]{:S(2)}, u32[]{:S(2)}) collective-permute-start(f32[392,16]{0,1:T(8,128)S(1)} %get-tuple-element.30), channel_id=1, source_target_pairs={{0,1},{1,2},{2,3},{3,4},{4,5},{5,6},{6,7},{7,8},{8,9},{9,10},{10,1... | collective-permute-start | bytes 75272 | tf_op jit(solution)/shard_map/ppermute | solution.py:13
  79.4 5.5 %collective-permute-start.15 = (f32[392,16]{0,1:T(8,128)S(1)}, f32[392,16]{0,1:T(8,128)S(1)}, u32[]{:S(2)}, u32[]{:S(2)}) collective-permute-start(f32[392,16]{0,1:T(8,128)S(1)} %get-tuple-element.31), channel_id=1, source_target_pairs={{1,0},{2,1},{3,2},{4,3},{5,4},{6,5},{7,6},{8,7},{9,8},{10,9},{11,1... | collective-permute-start | bytes 75272 | tf_op jit(solution)/shard_map/ppermute | solution.py:13
  80.7 139.5 %all-reduce.7.cloned.1.call-start = ((), (), s32[]{:S(2)}) async-start(), calls=%async_computation.1 | async-start | bytes 1064960 | tf_op jit(solution)/shard_map/psum | solution.py:77
  91.7 40.0 %collective-permute-start.8 = (f32[384,256]{1,0:T(8,128)}, f32[384,256]{1,0:T(8,128)}, u32[]{:S(2)}, u32[]{:S(2)}) collective-permute-start(f32[384,256]{1,0:T(8,128)} %get-tuple-element.12), channel_id=1, source_target_pairs={{0,16},{16,32},{32,48},{48,64},{64,80},{80,96},{96,112},{1,17},{17... | collective-permute-start | bytes 1179656 | tf_op jit(solution)/shard_map/ppermute | solution.py:13
  96.7 37.4 %collective-permute-start.10 = (f32[384,256]{1,0:T(8,128)}, f32[384,256]{1,0:T(8,128)}, u32[]{:S(2)}, u32[]{:S(2)}) collective-permute-start(f32[384,256]{1,0:T(8,128)} %get-tuple-element.13), channel_id=1, source_target_pairs={{0,1},{1,2},{2,3},{3,4},{4,5},{5,6},{6,7},{7,8},{8,9},{9,10},{10,1... | collective-permute-start | bytes 1179656 | tf_op jit(solution)/shard_map/ppermute | solution.py:13
  102.7 33.7 %collective-permute-start.11 = (f32[384,256]{1,0:T(8,128)S(1)}, f32[384,256]{1,0:T(8,128)}, u32[]{:S(2)}, u32[]{:S(2)}) collective-permute-start(f32[384,256]{1,0:T(8,128)S(1)} %get-tuple-element.14), channel_id=1, source_target_pairs={{1,0},{2,1},{3,2},{4,3},{5,4},{6,5},{7,6},{8,7},{9,8},{10,9},{11,1... | collective-permute-start | bytes 1179656 | tf_op jit(solution)/shard_map/ppermute | solution.py:13
  104.0 34.7 %collective-permute-start.9 = (f32[384,256]{1,0:T(8,128)S(1)}, f32[384,256]{1,0:T(8,128)}, u32[]{:S(2)}, u32[]{:S(2)}) collective-permute-start(f32[384,256]{1,0:T(8,128)S(1)} %get-tuple-element.15), channel_id=1, source_target_pairs={{16,0},{32,16},{48,32},{64,48},{80,64},{96,80},{112,96},{17,1},{33... | collective-permute-start | bytes 1179656 | tf_op jit(solution)/shard_map/ppermute | solution.py:13
  131.7 201.8 %all-reduce.9.cloned.1.call-start = ((), (), s32[]{:S(2)}) async-start(), calls=%async_computation.2 | async-start | bytes 1064960 | tf_op jit(solution)/shard_map/psum | solution.py:77
  233.8 7.5 %copy-start.24 = (f32[1536,256]{1,0:T(8,128)}, f32[1536,256]{1,0:T(8,128)S(1)}, u32[]{:S(2)}) copy-start(f32[1536,256]{1,0:T(8,128)S(1)} %fusion.9) | copy-start | bytes 4718596
  233.8 27.7 %slice-start.3 = ((s8[9437184]{0:T(1024)(128)(4,1)}), s8[4194304]{0:T(1024)(128)(4,1)S(1)}, s32[]{:S(2)}) async-start(s8[9437184]{0:T(1024)(128)(4,1)} %bitcast.174), calls=%async_computation.8 | async-start | bytes 8388608
  233.8 27.7 %slice-start.4 = ((s8[9437184]{0:T(1024)(128)(4,1)}), s8[4194304]{0:T(1024)(128)(4,1)S(1)}, s32[]{:S(2)}) async-start(s8[9437184]{0:T(1024)(128)(4,1)} %bitcast.174), calls=%async_computation.9 | async-start | bytes 8388608
  241.3 20.2 %slice-start.5 = ((s8[9437184]{0:T(1024)(128)(4,1)}), s8[1048576]{0:T(1024)(128)(4,1)S(1)}, s32[]{:S(2)}) async-start(s8[9437184]{0:T(1024)(128)(4,1)} %bitcast.174), calls=%async_computation.10 | async-start | bytes 2097152
  241.4 10.6 %collective-permute-start.16 = (f32[384,256]{1,0:T(8,128)S(1)}, f32[384,256]{1,0:T(8,128)S(1)}, u32[]{:S(2)}, u32[]{:S(2)}) collective-permute-start(f32[384,256]{1,0:T(8,128)S(1)} %get-tuple-element.8), channel_id=1, source_target_pairs={{0,16},{16,32},{32,48},{48,64},{64,80},{80,96},{96,112},{1,17},{17... | collective-permute-start | bytes 1179656 | tf_op jit(solution)/shard_map/ppermute | solution.py:13
  246.7 9.6 %collective-permute-start.18 = (f32[384,256]{1,0:T(8,128)S(1)}, f32[384,256]{1,0:T(8,128)S(1)}, u32[]{:S(2)}, u32[]{:S(2)}) collective-permute-start(f32[384,256]{1,0:T(8,128)S(1)} %get-tuple-element.9), channel_id=1, source_target_pairs={{0,1},{1,2},{2,3},{3,4},{4,5},{5,6},{6,7},{7,8},{8,9},{9,10},{10,1... | collective-permute-start | bytes 1179656 | tf_op jit(solution)/shard_map/ppermute | solution.py:13
  248.6 11.8 %collective-permute-start.19 = (f32[384,256]{1,0:T(8,128)S(1)}, f32[384,256]{1,0:T(8,128)S(1)}, u32[]{:S(2)}, u32[]{:S(2)}) collective-permute-start(f32[384,256]{1,0:T(8,128)S(1)} %get-tuple-element.10), channel_id=1, source_target_pairs={{1,0},{2,1},{3,2},{4,3},{5,4},{6,5},{7,6},{8,7},{9,8},{10,9},{11,1... | collective-permute-start | bytes 1179656 | tf_op jit(solution)/shard_map/ppermute | solution.py:13
  249.9 11.0 %collective-permute-start.17 = (f32[384,256]{1,0:T(8,128)S(1)}, f32[384,256]{1,0:T(8,128)S(1)}, u32[]{:S(2)}, u32[]{:S(2)}) collective-permute-start(f32[384,256]{1,0:T(8,128)S(1)} %get-tuple-element.11), channel_id=1, source_target_pairs={{16,0},{32,16},{48,32},{64,48},{80,64},{96,80},{112,96},{17,1},{33... | collective-permute-start | bytes 1179656 | tf_op jit(solution)/shard_map/ppermute | solution.py:13
  252.6 13.8 %copy-start.12 = (f32[384,256]{1,0:T(8,128)}, f32[384,256]{1,0:T(8,128)S(1)}, u32[]{:S(2)}) copy-start(f32[384,256]{1,0:T(8,128)S(1)} %convolution_subtract_fusion.11) | copy-start | bytes 1179652
  256.8 9.6 %copy-start.14 = (f32[384,256]{1,0:T(8,128)}, f32[384,256]{1,0:T(8,128)S(1)}, u32[]{:S(2)}) copy-start(f32[384,256]{1,0:T(8,128)S(1)} %convolution_subtract_fusion.9) | copy-start | bytes 1179652
  268.2 65.3 %copy-start.1 = (f32[1536,256]{1,0:T(8,128)S(1)}, f32[1536,256]{1,0:T(8,128)}, u32[]{:S(2)}) copy-start(f32[1536,256]{1,0:T(8,128)} %copy-done) | copy-start | bytes 4718596
  268.2 65.3 %collective-permute-start.20 = (f32[384,256]{1,0:T(8,128)}, f32[384,256]{1,0:T(8,128)}, u32[]{:S(2)}, u32[]{:S(2)}) collective-permute-start(f32[384,256]{1,0:T(8,128)} %get-tuple-element.4), channel_id=1, source_target_pairs={{0,16},{16,32},{32,48},{48,64},{64,80},{80,96},{96,112},{1,17},{17... | collective-permute-start | bytes 1179656 | tf_op jit(solution)/shard_map/ppermute | solution.py:13
  273.5 148.3 %all-reduce.11.cloned.1.call-start = ((), (), s32[]{:S(2)}) async-start(), calls=%async_computation.3 | async-start | bytes 1064960 | tf_op jit(solution)/shard_map/psum | solution.py:77
  273.5 62.3 %collective-permute-start.22 = (f32[384,256]{1,0:T(8,128)}, f32[384,256]{1,0:T(8,128)}, u32[]{:S(2)}, u32[]{:S(2)}) collective-permute-start(f32[384,256]{1,0:T(8,128)} %get-tuple-element.5), channel_id=1, source_target_pairs={{0,1},{1,2},{2,3},{3,4},{4,5},{5,6},{6,7},{7,8},{8,9},{9,10},{10,1... | collective-permute-start | bytes 1179656 | tf_op jit(solution)/shard_map/ppermute | solution.py:13
  277.2 61.0 %collective-permute-start.23 = (f32[384,256]{1,0:T(8,128)}, f32[384,256]{1,0:T(8,128)}, u32[]{:S(2)}, u32[]{:S(2)}) collective-permute-start(f32[384,256]{1,0:T(8,128)} %get-tuple-element.6), channel_id=1, source_target_pairs={{1,0},{2,1},{3,2},{4,3},{5,4},{6,5},{7,6},{8,7},{9,8},{10,9},{11,1... | collective-permute-start | bytes 1179656 | tf_op jit(solution)/shard_map/ppermute | solution.py:13
  278.5 62.0 %collective-permute-start.21 = (f32[384,256]{1,0:T(8,128)}, f32[384,256]{1,0:T(8,128)}, u32[]{:S(2)}, u32[]{:S(2)}) collective-permute-start(f32[384,256]{1,0:T(8,128)} %get-tuple-element.7), channel_id=1, source_target_pairs={{16,0},{32,16},{48,32},{64,48},{80,64},{96,80},{112,96},{17,1},{33... | collective-permute-start | bytes 1179656 | tf_op jit(solution)/shard_map/ppermute | solution.py:13
  (17 other events, 84.6 us)
Sparse Core Ops, SparseCore 0:
  69.7 61.9 all-reduce.4
  135.0 85.2 all-reduce.6
  273.6 59.8 all-reduce.8
  336.6 85.1 all-reduce.10
Sparse Core Ops, SparseCore 1:
  80.8 67.9 all-gather.2
